TPU v7x, 256 devices: a whole 4x4x8 slice. The times are simulated.
256 devices in a mesh: dp: 32 (over x, y, core), tensor: 8 (over z).
Axes of the slice: x: 4, y: 4, z: 8, core: 2. Of those that a mesh axis runs over, the one named last changes fastest.
Arguments:
- inputs: bfloat16 [32768, 8192], P('dp', 'tensor'), may hold values from -6 to 6
- frozen_value_weight: bfloat16 [8192, 1024], P('tensor'), may hold values from -0.0625 to 0.0625
- adapter_down_weight: bfloat16 [512, 8192, 64], P('dp', 'tensor'), may hold values from -0.0625 to 0.0625
- adapter_up_weight: bfloat16 [512, 64, 1024], P('dp', None, 'tensor'), may hold values from -0.75 to 0.75
- adapter_per_block: int32 [256], P('dp'), may hold values from 0 to 511, as said below
- adapter_storage_index: int32 [512], replicated, may hold values from 0 to 511, as said below
- value_gradient: bfloat16 [32768, 1024], P('dp', 'tensor'), may hold values from -6 to 6
Outputs:
- values: bfloat16 [32768, 1024], P('dp', 'tensor')
- grad_inputs: bfloat16 [32768, 8192], P('dp', 'tensor')
- grad_down: bfloat16 [512, 8192, 64], P('dp', 'tensor')
- grad_up: bfloat16 [512, 64, 1024], P('dp', None, 'tensor')
Inputs may be any that keep to these rules, and one draw needn't show every extreme that they name: Adapter a is kept by data device adapter_storage_index[a] // 16; adapter_storage_index is a permutation. `adapter_per_block`: the 8 blocks of one data device use adapters kept by pairwise different data devices; in every draw there is one data device whose adapters are used by a block of every data device, so that keeper serves all 32 data devices.
All inputs are finite; a program needn't handle non-finite values.
Results may differ from a plain program's by a relative error of at most 0.0054.
Values may be sent and summed in bfloat16 or wider, within the bound.
A program may use at most 128 MiB of HBM per device.

v0:
```python
import jax
import jax.numpy as jnp
from jax import lax
from jax.sharding import PartitionSpec as P

BLOCK = 128


adapter_scale = 0.5


def on_device(
    inputs,
    frozen_value_weight,
    adapter_down_weight,
    adapter_up_weight,
    adapter_per_block,
    adapter_storage_index,
    value_gradient,
):
    count_dp = lax.axis_size("dp")
    nblocks = adapter_per_block.shape[0]
    retained_rows = adapter_down_weight.shape[0]
    rows_per_worker = inputs.shape[0]
    feat = inputs.shape[1]
    column_range = value_gradient.shape[1]
    spot = adapter_storage_index[adapter_per_block]
    keeper = spot // retained_rows
    owner_ids = jnp.arange(count_dp, dtype=jnp.int32)
    match = keeper[None, :] == owner_ids[:, None]
    wanted = jnp.sum(jnp.where(match, spot[None, :] % retained_rows + 1, 0), axis=1) - 1
    asked = lax.all_to_all(wanted[:, None], "dp", split_axis=0, concat_axis=0, tiled=True)
    selected_adapter = (asked == jnp.arange(retained_rows, dtype=jnp.int32)[None, :]).astype(
        jnp.bfloat16
    )
    reply_down = jnp.einsum(
        "ig,gnx->inx", selected_adapter, adapter_down_weight, preferred_element_type=jnp.float32
    ).astype(jnp.bfloat16)
    returned_up_matrix = jnp.einsum(
        "cf,fxj->cxj", selected_adapter, adapter_up_weight, preferred_element_type=jnp.float32
    ).astype(jnp.bfloat16)
    fetched_down, fetched_up = (
        lax.all_to_all(reply_down, "dp", split_axis=0, concat_axis=0, tiled=True),
        lax.all_to_all(returned_up_matrix, "dp", split_axis=0, concat_axis=0, tiled=True),
    )
    block_down = jnp.take(fetched_down, keeper, axis=0)
    block_up = jnp.take(fetched_up, keeper, axis=0)
    x_blocks = inputs.reshape(nblocks, BLOCK, feat)
    low_part = jnp.einsum("bnd,bdr->bnr", x_blocks, block_down, preferred_element_type=jnp.float32)
    partial_base = jnp.dot(inputs, frozen_value_weight, preferred_element_type=jnp.float32)
    low = lax.psum(low_part, "tensor").astype(jnp.bfloat16)
    frozen_output = lax.psum_scatter(partial_base, "tensor", scatter_dimension=1, tiled=True)
    raised_output = jnp.einsum("bnr,brk->bnk", low, block_up, preferred_element_type=jnp.float32)
    values = (
        frozen_output + adapter_scale * raised_output.reshape(rows_per_worker, column_range)
    ).astype(jnp.bfloat16)
    dy_blocks = value_gradient.reshape(nblocks, BLOCK, column_range)
    partial_low_gradient = adapter_scale * jnp.einsum(
        "bnk,brk->bnr", dy_blocks, block_up, preferred_element_type=jnp.float32
    )
    low_rank_gradient = lax.psum(partial_low_gradient, "tensor").astype(jnp.bfloat16)
    grad_base = lax.dot_general(
        lax.all_gather(value_gradient, "tensor", axis=1, tiled=True),
        frozen_value_weight,
        (((1,), (1,)), ((), ())),
        preferred_element_type=jnp.float32,
    )
    back = jnp.einsum(
        "bnr,bdr->bnd", low_rank_gradient, block_down, preferred_element_type=jnp.float32
    )
    grad_inputs = (grad_base + back.reshape(rows_per_worker, feat)).astype(jnp.bfloat16)
    route = match.astype(jnp.bfloat16)
    term_down = jnp.einsum(
        "bnd,bnr->bdr", x_blocks, low_rank_gradient, preferred_element_type=jnp.float32
    ).astype(jnp.bfloat16)
    term_up = jnp.einsum("bnr,bnk->brk", low, dy_blocks, preferred_element_type=jnp.float32).astype(
        jnp.bfloat16
    )
    send_down = jnp.einsum(
        "ob,bdr->odr", route, term_down, preferred_element_type=jnp.float32
    ).astype(jnp.bfloat16)
    send_up = jnp.einsum("ob,brk->ork", route, term_up, preferred_element_type=jnp.float32).astype(
        jnp.bfloat16
    )
    got_down, got_up = (
        lax.all_to_all(send_down, "dp", split_axis=0, concat_axis=0, tiled=True),
        lax.all_to_all(send_up, "dp", split_axis=0, concat_axis=0, tiled=True),
    )
    grad_down = jnp.einsum(
        "sa,sdr->adr", selected_adapter, got_down, preferred_element_type=jnp.float32
    ).astype(jnp.bfloat16)
    grad_up = jnp.einsum(
        "sa,srk->ark", selected_adapter, got_up, preferred_element_type=jnp.float32
    ).astype(jnp.bfloat16)
    return (values, grad_inputs, grad_down, grad_up)


def solution(mesh):
    return jax.shard_map(
        on_device,
        mesh=mesh,
        in_specs=(
            P("dp", "tensor"),
            P("tensor", None),
            P("dp", "tensor", None),
            P("dp", None, "tensor"),
            P("dp"),
            P(),
            P("dp", "tensor"),
        ),
        out_specs=(
            P("dp", "tensor"),
            P("dp", "tensor"),
            P("dp", "tensor", None),
            P("dp", None, "tensor"),
        ),
        check_vma=False,
    )
```

profile of v0, /device:TPU:1, one launch (start us, length us, event | category | flops | bytes accessed | tf_op | source)
XLA Modules:
  0.0 241.1 jit_solution(14531232529072332693)
XLA Ops:
  7.2 0.0 copy-start
  7.2 0.0 all-gather.2.cloned.1.call-start
  7.2 0.7 all-gather.2.cloned.1.call-update
  7.9 0.7 compare_select_fusion.2
  8.6 1.3 gather_fusion
  9.9 0.1 select_reduce_fusion
  10.0 0.1 copy.38
  10.1 15.3 %all_to_all.26 = s32[32,1,1]{2,1,0:T(1,128)S(1)} all-to-all(s32[32,1,1]{2,1,0:T(1,128)S(1)} %copy.38), channel_id=1, replica_groups=mesh['dp'=32,'tensor'=8] {'dp'}, dimensions={0} | all-to-all | bytes 256 | tf_op jit(solution)/shard_map/all_to_all | solution.py:32
  25.4 0.7 reduce
  26.1 1.3 convolution_convert_fusion.3
  27.4 1.0 copy.42
  28.4 4.2 %all-to-all-start.2 = ((bf16[32,64,128]{2,1,0:T(8,128)(2,1)}), bf16[32,64,128]{2,1,0:T(8,128)(2,1)S(1)}, u32[]{:S(2)}, u32[]{:S(2)}) async-start(bf16[32,64,128]{2,1,0:T(8,128)(2,1)} %copy.42), calls=%async_computation.3 | async-start | bytes 1048576 | tf_op jit(solution)/shard_map/all_to_all | solution.py:44
  32.6 3.3 %convolution_convert_fusion.1 = bf16[32,1024,64]{1,0,2:T(8,128)(2,1)S(1)} fusion(bf16[16,1024,64]{1,2,0:T(8,128)(2,1)} %param.9, s32[32]{0:T(128)S(1)} %reduce), kind=kOutput, calls=%fused_computation.8 | convolution fusion | flops 69206528 | bytes 6291584 | tf_op jit(solution)/shard_map/ig,gnx->inx/dot_general | solution.py:36
  35.9 4.3 %copy.40 = bf16[32,1024,64]{1,2,0:T(8,128)(2,1)} copy(bf16[32,1024,64]{1,0,2:T(8,128)(2,1)S(1)} %convolution_convert_fusion.1) | data formatting | bytes 8388608 | tf_op jit(solution)/shard_map/convert_element_type | solution.py:38
  40.2 4.1 %all-to-all-done.2 = bf16[32,64,128]{2,1,0:T(8,128)(2,1)S(1)} async-done(((bf16[32,64,128]{2,1,0:T(8,128)(2,1)}), bf16[32,64,128]{2,1,0:T(8,128)(2,1)S(1)}, u32[]{:S(2)}, u32[]{:S(2)}) %all-to-all-start.2) | async-done | bytes 524320 | tf_op jit(solution)/shard_map/all_to_all | solution.py:44
  44.4 4.6 %all-to-all-start.1 = ((bf16[32,1024,64]{1,2,0:T(8,128)(2,1)}), bf16[32,1024,64]{1,2,0:T(8,128)(2,1)}, u32[]{:S(2)}, u32[]{:S(2)}) async-start(bf16[32,1024,64]{1,2,0:T(8,128)(2,1)} %copy.40), calls=%async_computation.2 | async-start | bytes 8388608 | tf_op jit(solution)/shard_map/all_to_all | solution.py:43
  49.0 0.0 reduce-scatter.2.cloned.1.call-start
  49.1 0.0 copy-done
  49.1 5.9 %fusion.39 = f32[1024,1024]{1,0:T(8,128)} fusion(bf16[1024,1024]{1,0:T(8,128)(2,1)S(1)} %copy-done, bf16[1024,1024]{1,0:T(8,128)(2,1)} %param.8), kind=kOutput, calls=%fused_computation.68 | convolution fusion | flops 2147483648 | bytes 8388608 | tf_op jit(solution)/shard_map/dot_general | solution.py:50
  55.0 0.0 reduce-scatter.2.cloned.1.call-update
  55.0 0.6 gather_fusion.2
  55.6 0.3 copy-done.1
  55.9 1.0 fusion.8
  56.9 44.0 %all-to-all-done.1 = bf16[32,1024,64]{1,2,0:T(8,128)(2,1)} async-done(((bf16[32,1024,64]{1,2,0:T(8,128)(2,1)}), bf16[32,1024,64]{1,2,0:T(8,128)(2,1)}, u32[]{:S(2)}, u32[]{:S(2)}) %all-to-all-start.1) | async-done | bytes 4194336 | tf_op jit(solution)/shard_map/all_to_all | solution.py:43
  100.9 2.8 %gather_fusion.1 = bf16[8,1024,64]{1,2,0:T(8,128)(2,1)S(1)} fusion(bf16[32,1024,64]{1,2,0:T(8,128)(2,1)} %all-to-all-done.1, s32[1024]{0:T(1024)S(1)} %pad_clamp_fusion), kind=kCustom, calls=%fused_computation.1 | custom fusion | bytes 2097184 | tf_op jit(solution)/shard_map/jit(_take)/gather | solution.py:46
  103.7 1.6 convolution_bitcast_fusion
  105.3 34.4 %all-reduce.2 = (bf16[8,128,64]{1,2,0:T(8,128)(2,1)}, bf16[8,128,64]{1,2,0:T(8,128)(2,1)}) all-reduce(f32[8,128,64]{1,2,0:T(8,128)} %convolution_bitcast_fusion, f32[8,128,64]{1,2,0:T(8,128)} %fusion.8), channel_id=1, replica_groups=mesh['dp'=32,'tensor'=8] {'tensor'}, use_global_device_ids=true, to_apply=%region_2.3 | all-reduce | flops 131072 | bytes 786432 | tf_op jit(solution)/shard_map/psum | solution.py:51
  139.7 1.1 convolution_convert_fusion.6
  140.8 0.0 copy-start.3
  140.8 0.4 convolution_convert_fusion.4
  141.3 1.0 copy.47
  142.3 12.8 %all-to-all-start.4 = ((bf16[32,64,128]{2,1,0:T(8,128)(2,1)}), bf16[32,64,128]{2,1,0:T(8,128)(2,1)}, u32[]{:S(2)}, u32[]{:S(2)}) async-start(bf16[32,64,128]{2,1,0:T(8,128)(2,1)} %copy.47), calls=%async_computation.5 | async-start | bytes 1048576 | tf_op jit(solution)/shard_map/all_to_all | solution.py:87
  155.1 0.0 copy-done.3
  155.1 0.4 fusion.7
  155.5 1.4 convolution_convert_fusion
  156.9 4.3 %copy.44 = bf16[32,1024,64]{1,2,0:T(8,128)(2,1)} copy(bf16[32,1024,64]{1,0,2:T(8,128)(2,1)S(1)} %convolution_convert_fusion) | data formatting | bytes 8388608 | tf_op jit(solution)/shard_map/convert_element_type | solution.py:81
  161.2 5.5 %all-to-all-done.4 = bf16[32,64,128]{2,1,0:T(8,128)(2,1)} async-done(((bf16[32,64,128]{2,1,0:T(8,128)(2,1)}), bf16[32,64,128]{2,1,0:T(8,128)(2,1)}, u32[]{:S(2)}, u32[]{:S(2)}) %all-to-all-start.4) | async-done | bytes 524320 | tf_op jit(solution)/shard_map/all_to_all | solution.py:87
  166.7 4.6 %all-to-all-start.3 = ((bf16[32,1024,64]{1,2,0:T(8,128)(2,1)}), bf16[32,1024,64]{1,2,0:T(8,128)(2,1)}, u32[]{:S(2)}, u32[]{:S(2)}) async-start(bf16[32,1024,64]{1,2,0:T(8,128)(2,1)} %copy.44), calls=%async_computation.4 | async-start | bytes 8388608 | tf_op jit(solution)/shard_map/all_to_all | solution.py:86
  171.4 0.0 copy-done.4
  171.4 1.1 convolution_multiply_fusion
  172.5 2.7 %fusion.12 = f32[8,128,1024]{2,1,0:T(8,128)} fusion(bf16[8,1024,64]{1,2,0:T(8,128)(2,1)S(1)} %gather_fusion.1, pred[8]{0:T(512)(128)(4,1)S(1)} %get-tuple-element.22, bf16[8,128,64]{1,2,0:T(8,128)(2,1)S(1)} %copy-done.3), kind=kOutput, calls=%fused_computation.26 | convolution fusion | flops 134742016 | bytes 5373960 | tf_op jit(solution)/shard_map/bnr,bdr->bnd/dot_general | solution.py:68
  175.2 7.2 %fusion = bf16[1024,1024]{1,0:T(8,128)(2,1)} fusion(f32[8,128,1024]{2,1,0:T(8,128)} %fusion.12, bf16[1024,1024]{1,0:T(8,128)(2,1)} %all-gather.2.cloned.1.call-done, bf16[1024,1024]{1,0:T(8,128)(2,1)} %param.8), kind=kOutput, calls=%fused_computation.4 | convolution fusion | flops 2149580800 | bytes 10485760 | tf_op jit(solution)/shard_map/dot_general | solution.py:62
  182.4 1.4 convolution_convert_fusion.5
  183.8 0.8 copy.50
  184.6 38.7 %all-to-all-done.3 = bf16[32,1024,64]{1,2,0:T(8,128)(2,1)} async-done(((bf16[32,1024,64]{1,2,0:T(8,128)(2,1)}), bf16[32,1024,64]{1,2,0:T(8,128)(2,1)}, u32[]{:S(2)}, u32[]{:S(2)}) %all-to-all-start.3) | async-done | bytes 4194336 | tf_op jit(solution)/shard_map/all_to_all | solution.py:86
  223.2 6.8 %fusion.4 = bf16[16,1024,64]{1,0,2:T(8,128)(2,1)S(1)} fusion(bf16[32,1024,64]{1,2,0:T(8,128)(2,1)} %all-to-all-done.3, s32[32]{0:T(128)S(1)} %reduce), kind=kOutput, calls=%fused_computation.10 | convolution fusion | flops 68157952 | bytes 6291584 | tf_op jit(solution)/shard_map/sa,sdr->adr/dot_general | solution.py:89
  230.0 2.5 %copy.49 = bf16[16,1024,64]{1,2,0:T(8,128)(2,1)} copy(bf16[16,1024,64]{1,0,2:T(8,128)(2,1)S(1)} %fusion.4) | data formatting | bytes 4194304
  232.5 1.8 fusion.10
  (12 shorter events, 0.1 us)
Async XLA Ops:
  7.2 41.9 %copy-start = (bf16[1024,1024]{1,0:T(8,128)(2,1)S(1)}, bf16[1024,1024]{1,0:T(8,128)(2,1)}, u32[]{:S(2)}) copy-start(bf16[1024,1024]{1,0:T(8,128)(2,1)} %param.7) | copy-start | bytes 6291460
  7.2 168.0 %all-gather.2.cloned.1.call-start = ((), (), s32[]{:S(2)}) async-start(), calls=%async_computation.7 | async-start | bytes 2359296 | tf_op jit(solution)/shard_map/all_gather | solution.py:63
  28.4 15.9 %all-to-all-start.2 = ((bf16[32,64,128]{2,1,0:T(8,128)(2,1)}), bf16[32,64,128]{2,1,0:T(8,128)(2,1)S(1)}, u32[]{:S(2)}, u32[]{:S(2)}) async-start(bf16[32,64,128]{2,1,0:T(8,128)(2,1)} %copy.42), calls=%async_computation.3 | async-start | bytes 1048576 | tf_op jit(solution)/shard_map/all_to_all | solution.py:44
  44.4 56.5 %all-to-all-start.1 = ((bf16[32,1024,64]{1,2,0:T(8,128)(2,1)}), bf16[32,1024,64]{1,2,0:T(8,128)(2,1)}, u32[]{:S(2)}, u32[]{:S(2)}) async-start(bf16[32,1024,64]{1,2,0:T(8,128)(2,1)} %copy.40), calls=%async_computation.2 | async-start | bytes 8388608 | tf_op jit(solution)/shard_map/all_to_all | solution.py:43
  49.0 183.5 %reduce-scatter.2.cloned.1.call-start = ((), (), s32[]{:S(2)}) async-start(), calls=%async_computation.6 | async-start | bytes 4718592 | tf_op jit(solution)/shard_map/reduce_scatter | solution.py:52
  55.0 0.9 copy-start.1
  140.8 14.2 %copy-start.3 = (bf16[8,128,64]{1,2,0:T(8,128)(2,1)S(1)}, bf16[8,128,64]{1,2,0:T(8,128)(2,1)}, u32[]{:S(2)}) copy-start(bf16[8,128,64]{1,2,0:T(8,128)(2,1)} %get-tuple-element.21) | copy-start | bytes 393220
  142.3 24.5 %all-to-all-start.4 = ((bf16[32,64,128]{2,1,0:T(8,128)(2,1)}), bf16[32,64,128]{2,1,0:T(8,128)(2,1)}, u32[]{:S(2)}, u32[]{:S(2)}) async-start(bf16[32,64,128]{2,1,0:T(8,128)(2,1)} %copy.47), calls=%async_computation.5 | async-start | bytes 1048576 | tf_op jit(solution)/shard_map/all_to_all | solution.py:87
  161.2 10.2 %copy-start.4 = (bf16[8,128,64]{1,2,0:T(8,128)(2,1)S(1)}, bf16[8,128,64]{1,2,0:T(8,128)(2,1)}, u32[]{:S(2)}) copy-start(bf16[8,128,64]{1,2,0:T(8,128)(2,1)} %get-tuple-element.20) | copy-start | bytes 393220
  166.7 56.5 %all-to-all-start.3 = ((bf16[32,1024,64]{1,2,0:T(8,128)(2,1)}), bf16[32,1024,64]{1,2,0:T(8,128)(2,1)}, u32[]{:S(2)}, u32[]{:S(2)}) async-start(bf16[32,1024,64]{1,2,0:T(8,128)(2,1)} %copy.44), calls=%async_computation.4 | async-start | bytes 8388608 | tf_op jit(solution)/shard_map/all_to_all | solution.py:86
  230.0 2.5 %copy-start.2 = (f32[8,128,128]{2,1,0:T(8,128)S(1)}, f32[8,128,128]{2,1,0:T(8,128)}, u32[]{:S(2)}) copy-start(f32[8,128,128]{2,1,0:T(8,128)} %convolution_multiply_fusion) | copy-start | bytes 1572868
Sparse Core Ops, SparseCore 0:
  9.7 47.2 all-gather.1
  59.6 59.0 reduce-scatter.1
where the time goes:
time: 244 us; the launch traced here: 241 us
  waiting for transfers between devices  93 us (38%)
  blocking collectives  49.7 us (20%)
  matrix products  35.6 us (15%)
  starting transfers between devices  26.4 us (11%)
  local copies, waits for them, and re-layouts  19 us (8%)
  between operations  14.2 us (6%)
  other arithmetic  3.25 us (1%)
    all_to_all x1, waiting for transfers between devices, on_device(): lax.all_to_all(reply_down, 'dp', split_axis=0, concat_axis=0, tiled=True)  44 us
    all_to_all x1, waiting for transfers between devices, on_device(): lax.all_to_all(send_down, 'dp', split_axis=0, concat_axis=0, tiled=True)  38.7 us
    psum x1, blocking collectives, on_device(): low = lax.psum(low_part, 'tensor').astype(jnp.bfloat16)  34.4 us
    all_to_all x1, blocking collectives, on_device(): lax.all_to_all(wanted[:, None], 'dp', split_axis=0, concat_axis=0, tiled=...  15.3 us
    all_to_all x1, starting transfers between devices, on_device(): lax.all_to_all(send_up, 'dp', split_axis=0, concat_axis=0, tiled=True)  12.8 us
    dot_general x1, matrix products, on_device(): lax.dot_general(lax.all_gather(value_gradient, 'tensor', axis=1, tiled=Tr...  7.15 us
    dot_general x1, matrix products, on_device(): jnp.einsum('sa,sdr->adr', selected_adapter, got_down, preferred_element_t...  6.78 us
    dot_general x1, matrix products, on_device(): jnp.dot(inputs, frozen_value_weight, preferred_element_type=jnp.float32)  5.88 us
  transfers between devices with their start and end apart: 6, of which 4 were waited for; matrix products, arithmetic and copies ran while one was open for 23% of the time, Pallas kernels for 0%

commit v1 on v0

v1 whole, which is shorter than its diff:
```python
import jax
import jax.numpy as jnp
from jax import lax
from jax.sharding import PartitionSpec as P

BLOCK = 128


adapter_scale = 0.5


def exchange(pieces):
    return lax.all_to_all(pieces, "dp", split_axis=0, concat_axis=0, tiled=True)


def cut(mats, parts):
    m, rank, width = mats.shape
    rows = rank // parts
    return mats.reshape(m, parts, rows * width).swapaxes(0, 1)


def join(pieces, width):
    parts, m, size = pieces.shape
    return pieces.swapaxes(0, 1).reshape(m, parts * (size // width), width)


def on_device(
    inputs,
    frozen_value_weight,
    adapter_down_weight,
    adapter_up_weight,
    adapter_per_block,
    adapter_storage_index,
    value_gradient,
):
    n = lax.axis_size("dp")
    nblocks = adapter_per_block.shape[0]
    kept = adapter_down_weight.shape[0]
    total = adapter_storage_index.shape[0]
    rows = inputs.shape[0]
    feat = inputs.shape[1]
    columns = value_gradient.shape[1]
    f32, bf16 = jnp.float32, jnp.bfloat16

    up_table = exchange(cut(adapter_up_weight, n)).reshape(total, -1)
    down_table = exchange(cut(adapter_down_weight.swapaxes(1, 2), n)).reshape(total, -1)

    spot = adapter_storage_index[adapter_per_block]
    spots = lax.all_gather(spot, "dp", axis=0, tiled=True)
    pick = (spots[:, None] == jnp.arange(total, dtype=jnp.int32)[None, :]).astype(bf16)

    def fetch(table, width):
        chosen = jnp.dot(pick, table, preferred_element_type=f32).astype(bf16)
        return join(exchange(chosen.reshape(n, nblocks, -1)), width)

    def give(terms, width):
        pieces = exchange(cut(terms, n)).reshape(n * nblocks, -1)
        sums = lax.dot_general(
            pick, pieces, (((0,), (0,)), ((), ())), preferred_element_type=f32
        ).astype(bf16)
        return join(exchange(sums.reshape(n, kept, -1)), width)

    block_up = fetch(up_table, columns)
    block_down = fetch(down_table, feat)

    x_blocks = inputs.reshape(nblocks, BLOCK, feat)
    dy_blocks = value_gradient.reshape(nblocks, BLOCK, columns)

    partial_low_gradient = adapter_scale * jnp.einsum(
        "bnk,brk->bnr", dy_blocks, block_up, preferred_element_type=f32
    )
    low_rank_gradient = lax.psum(partial_low_gradient, "tensor").astype(bf16)
    term_down = jnp.einsum(
        "bnd,bnr->brd", x_blocks, low_rank_gradient, preferred_element_type=f32
    ).astype(bf16)
    grad_down = give(term_down, feat).swapaxes(1, 2)

    partial_base = jnp.dot(inputs, frozen_value_weight, preferred_element_type=f32)
    frozen_output = lax.psum_scatter(partial_base, "tensor", scatter_dimension=1, tiled=True)
    low_part = jnp.einsum("bnd,brd->bnr", x_blocks, block_down, preferred_element_type=f32)
    low = lax.psum(low_part, "tensor").astype(bf16)
    term_up = jnp.einsum("bnr,bnk->brk", low, dy_blocks, preferred_element_type=f32).astype(bf16)
    grad_up = give(term_up, columns)

    raised_output = jnp.einsum("bnr,brk->bnk", low, block_up, preferred_element_type=f32)
    values = (frozen_output + adapter_scale * raised_output.reshape(rows, columns)).astype(bf16)
    grad_base = lax.dot_general(
        lax.all_gather(value_gradient, "tensor", axis=1, tiled=True),
        frozen_value_weight,
        (((1,), (1,)), ((), ())),
        preferred_element_type=f32,
    )
    back = jnp.einsum("bnr,brd->bnd", low_rank_gradient, block_down, preferred_element_type=f32)
    grad_inputs = (grad_base + back.reshape(rows, feat)).astype(bf16)
    return (values, grad_inputs, grad_down, grad_up)


def solution(mesh):
    return jax.shard_map(
        on_device,
        mesh=mesh,
        in_specs=(
            P("dp", "tensor"),
            P("tensor", None),
            P("dp", "tensor", None),
            P("dp", None, "tensor"),
            P("dp"),
            P(),
            P("dp", "tensor"),
        ),
        out_specs=(
            P("dp", "tensor"),
            P("dp", "tensor"),
            P("dp", "tensor", None),
            P("dp", None, "tensor"),
        ),
        check_vma=False,
    )
```

time: 244 us -> 260 us (1.066)
  waiting for transfers between devices: 93 us -> 57 us
  starting transfers between devices: 26.4 us -> 52.5 us
  blocking collectives: 49.7 us -> 65.2 us
  local copies, waits for them, and re-layouts: 19 us -> 32.6 us
    all_to_all x4 -> x8, waiting for transfers between devices: 92.3 us -> 56.3 us  [exchange(): return lax.all_to_all(pieces, 'dp', split_axis=0, concat_axis=0, tiled=True)]
    unnamed x0 -> x1, blocking collectives: none -> 31.7 us
    all_to_all x4 -> x8, starting transfers between devices: 26.3 us -> 52.5 us  [exchange(): return lax.all_to_all(pieces, 'dp', split_axis=0, concat_axis=0, tiled=True)]
    reshape x0 -> x10, local copies, waits for them, and re-layouts: none -> 18.1 us  [the longest x6 10.8 us: cut(): return mats.reshape(m, parts, rows * width).swapaxes(0, 1)]
    all_to_all x1 -> x0, blocking collectives: 15.3 us -> none  [on_device(): lax.all_to_all(wanted[:, None], 'dp', split_axis=0, concat_axis=0, tiled=...]
    transpose x0 -> x6, local copies, waits for them, and re-layouts: none -> 11.3 us  [the longest x4 6.4 us: join(): return pieces.swapaxes(0, 1).reshape(m, parts * (size // width), width)]
    convert_element_type x4 -> x0, local copies, waits for them, and re-layouts: 10.6 us -> none  [the longest x1 4.3 us: on_device(): reply_down = jnp.einsum('ig,gnx->inx', selected_adapter, adapter_down_wei...]
    gather x2 -> x0, local copies, waits for them, and re-layouts: 3.42 us -> none  [the longest x1 2.85 us: on_device(): block_down = jnp.take(fetched_down, keeper, axis=0)]
  transfers between devices with their start and end apart: 6 -> 10, of which waited for: 4 -> 7; matrix products, arithmetic and copies ran while one was open for 23% -> 25% of each run, Pallas kernels for 0% -> 0%
where the time goes in v1:
time: 260 us; the launch traced here: 258 us
  blocking collectives  65.2 us (25%)
  waiting for transfers between devices  57 us (22%)
  starting transfers between devices  52.5 us (20%)
  matrix products  34 us (13%)
  local copies, waits for them, and re-layouts  32.6 us (13%)
  between operations  14.9 us (6%)
    all_to_all x8, waiting for transfers between devices, exchange(): return lax.all_to_all(pieces, 'dp', split_axis=0, concat_axis=0, tiled=True)  56.3 us
    all_to_all x8, starting transfers between devices, exchange(): return lax.all_to_all(pieces, 'dp', split_axis=0, concat_axis=0, tiled=True)  52.5 us
    psum x1, blocking collectives, on_device(): low = lax.psum(low_part, 'tensor').astype(bf16)  33.5 us
    unnamed x1, blocking collectives  31.7 us
    reshape x6, local copies, waits for them, and re-layouts, cut(): return mats.reshape(m, parts, rows * width).swapaxes(0, 1)  10.8 us
    reshape x4, local copies, waits for them, and re-layouts, join(): return pieces.swapaxes(0, 1).reshape(m, parts * (size // width), width)  7.29 us
    dot_general x1, matrix products, on_device(): lax.dot_general(lax.all_gather(value_gradient, 'tensor', axis=1, tiled=Tr...  7.15 us
    transpose x4, local copies, waits for them, and re-layouts, join(): return pieces.swapaxes(0, 1).reshape(m, parts * (size // width), width)  6.4 us
  transfers between devices with their start and end apart: 10, of which 7 were waited for; matrix products, arithmetic and copies ran while one was open for 25% of the time, Pallas kernels for 0%

profile of v1, /device:TPU:1, one launch (start us, length us, event | category | flops | bytes accessed | tf_op | source)
XLA Modules:
  0.0 258.1 jit_solution(17837545737444184201)
XLA Ops:
  7.2 0.7 all-gather.3.cloned.1.call-update
  8.0 0.8 copy-done
  8.8 5.9 %fusion.16 = f32[1024,1024]{1,0:T(8,128)} fusion(bf16[1024,1024]{1,0:T(8,128)(2,1)S(1)} %copy-done, bf16[1024,1024]{1,0:T(8,128)(2,1)} %param.8), kind=kOutput, calls=%fused_computation.33 | convolution fusion | flops 2147483648 | bytes 8388608 | tf_op jit(solution)/shard_map/dot_general | solution.py:78
  14.7 0.9 copy-done.4
  15.7 0.9 copy.31
  16.5 8.6 %all-to-all-start.2 = ((bf16[32,16,256]{2,1,0:T(8,128)(2,1)}), bf16[32,16,256]{2,1,0:T(8,128)(2,1)S(1)}, u32[]{:S(2)}, u32[]{:S(2)}) async-start(bf16[32,16,256]{2,1,0:T(8,128)(2,1)} %copy.31), calls=%async_computation.3 | async-start | bytes 524288 | tf_op jit(solution)/shard_map/all_to_all | solution.py:13
  25.1 4.1 %reshape.69 = bf16[16,32,2048]{2,1,0:T(8,128)(2,1)} reshape(bf16[16,64,1024]{2,1,0:T(8,128)(2,1)} %bitcast.69) | data formatting | bytes 4194304 | tf_op jit(solution)/shard_map/reshape | solution.py:19
  29.2 4.1 %copy.29 = bf16[32,16,2048]{2,1,0:T(8,128)(2,1)} copy(bf16[32,16,2048]{2,0,1:T(8,128)(2,1)} %bitcast.64) | data formatting | bytes 4194304 | tf_op jit(solution)/shard_map/transpose | solution.py:19
  33.3 0.9 all-to-all-done.2
  34.1 6.7 %all-to-all-start = ((bf16[32,16,2048]{2,1,0:T(8,128)(2,1)}), bf16[32,16,2048]{2,1,0:T(8,128)(2,1)}, u32[]{:S(2)}, u32[]{:S(2)}) async-start(bf16[32,16,2048]{2,1,0:T(8,128)(2,1)} %copy.29), calls=%async_computation.1 | async-start | bytes 4194304 | tf_op jit(solution)/shard_map/all_to_all | solution.py:13
  40.9 0.6 gather_fusion
  41.6 0.6 dynamic-slice
  43.0 31.7 %all-reduce = s32[256]{0:T(256)S(1)} all-reduce(s32[256]{0:T(256)S(1)} %dynamic-update-slice), channel_id=2, replica_groups=mesh['dp'=32,'tensor'=8] {'dp'}, use_global_device_ids=true, to_apply=%add | all-reduce | flops 256 | bytes 2048
  74.8 0.9 fusion.3
  75.7 6.9 %all-to-all-start.3 = ((bf16[32,8,256]{2,1,0:T(8,128)(2,1)}), bf16[32,8,256]{2,1,0:T(8,128)(2,1)S(1)}, u32[]{:S(2)}, u32[]{:S(2)}) async-start(bf16[32,8,256]{2,1,0:T(8,128)(2,1)} %fusion.3), calls=%async_computation.4 | async-start | bytes 262144 | tf_op jit(solution)/shard_map/all_to_all | solution.py:13
  82.6 3.3 %fusion.1 = bf16[32,8,2048]{2,1,0:T(8,128)(2,1)} fusion(bf16[512,2048]{1,0:T(8,128)(2,1)} %bitcast.3, s32[256]{0:T(256)S(1)} %all-reduce), kind=kOutput, calls=%fused_computation.5 | convolution fusion | flops 537526272 | bytes 3146752 | tf_op jit(solution)/shard_map/dot_general | solution.py:53
  85.9 4.5 %all-to-all-done.3 = bf16[32,8,256]{2,1,0:T(8,128)(2,1)S(1)} async-done(((bf16[32,8,256]{2,1,0:T(8,128)(2,1)}), bf16[32,8,256]{2,1,0:T(8,128)(2,1)S(1)}, u32[]{:S(2)}, u32[]{:S(2)}) %all-to-all-start.3) | async-done | bytes 131104 | tf_op jit(solution)/shard_map/all_to_all | solution.py:13
  90.4 4.0 %all-to-all-start.1 = ((bf16[32,8,2048]{2,1,0:T(8,128)(2,1)}), bf16[32,8,2048]{2,1,0:T(8,128)(2,1)S(1)}, u32[]{:S(2)}, u32[]{:S(2)}) async-start(bf16[32,8,2048]{2,1,0:T(8,128)(2,1)} %fusion.1), calls=%async_computation.2 | async-start | bytes 2097152 | tf_op jit(solution)/shard_map/all_to_all | solution.py:13
  94.4 0.7 copy.32
  95.1 1.0 reshape.77
  96.1 1.0 fusion.2
  97.1 14.4 %all-to-all-done.1 = bf16[32,8,2048]{2,1,0:T(8,128)(2,1)S(1)} async-done(((bf16[32,8,2048]{2,1,0:T(8,128)(2,1)}), bf16[32,8,2048]{2,1,0:T(8,128)(2,1)S(1)}, u32[]{:S(2)}, u32[]{:S(2)}) %all-to-all-start.1) | async-done | bytes 1048608 | tf_op jit(solution)/shard_map/all_to_all | solution.py:13
  111.4 1.5 copy.30
  113.0 1.4 reshape.72
  114.4 1.5 convolution_bitcast_fusion
  115.9 33.5 %all-reduce.3 = (bf16[8,128,64]{1,2,0:T(8,128)(2,1)}, bf16[8,128,64]{1,2,0:T(8,128)(2,1)}) all-reduce(f32[8,128,64]{1,2,0:T(8,128)} %convolution_bitcast_fusion, f32[8,128,64]{1,2,0:T(8,128)} %fusion.2), channel_id=1, replica_groups=mesh['dp'=32,'tensor'=8] {'tensor'}, use_global_device_ids=true, to_apply=%region_1.0 | all-reduce | flops 131072 | bytes 786432 | tf_op jit(solution)/shard_map/psum | solution.py:81
  149.5 1.8 convolution_convert_fusion.4
  151.2 1.0 reshape.84
  152.2 0.7 copy.40
  152.9 10.8 %all-to-all-start.6 = ((bf16[32,8,256]{2,1,0:T(8,128)(2,1)}), bf16[32,8,256]{2,1,0:T(8,128)(2,1)S(1)}, u32[]{:S(2)}, u32[]{:S(2)}) async-start(bf16[32,8,256]{2,1,0:T(8,128)(2,1)} %bitcast.60), calls=%async_computation.7 | async-start | bytes 262144 | tf_op jit(solution)/shard_map/all_to_all | solution.py:13
  163.7 2.3 convolution_convert_fusion.2
  166.0 2.2 reshape.80
  168.2 2.8 %copy.39 = bf16[8,32,2048]{2,0,1:T(8,128)(2,1)} copy(bf16[8,32,2048]{2,1,0:T(8,128)(2,1)} %reshape.80) | data formatting | bytes 2097152 | tf_op jit(solution)/shard_map/reshape | solution.py:19
  171.4 7.0 %all-to-all-start.4 = ((bf16[32,8,2048]{2,1,0:T(8,128)(2,1)}), bf16[32,8,2048]{2,1,0:T(8,128)(2,1)}, u32[]{:S(2)}, u32[]{:S(2)}) async-start(bf16[32,8,2048]{2,1,0:T(8,128)(2,1)} %bitcast.66), calls=%async_computation.5 | async-start | bytes 2097152 | tf_op jit(solution)/shard_map/all_to_all | solution.py:13
  178.4 1.1 convolution_convert_fusion.3
  179.5 15.8 %all-to-all-done.4 = bf16[32,8,2048]{2,1,0:T(8,128)(2,1)} async-done(((bf16[32,8,2048]{2,1,0:T(8,128)(2,1)}), bf16[32,8,2048]{2,1,0:T(8,128)(2,1)}, u32[]{:S(2)}, u32[]{:S(2)}) %all-to-all-start.4) | async-done | bytes 1048608 | tf_op jit(solution)/shard_map/all_to_all | solution.py:13
  195.4 4.0 %all-to-all-start.7 = ((bf16[32,16,256]{2,1,0:T(8,128)(2,1)}), bf16[32,16,256]{2,1,0:T(8,128)(2,1)S(1)}, u32[]{:S(2)}, u32[]{:S(2)}) async-start(bf16[32,16,256]{2,1,0:T(8,128)(2,1)} %bitcast.72), calls=%async_computation.8 | async-start | bytes 524288 | tf_op jit(solution)/shard_map/all_to_all | solution.py:13
  199.3 3.4 %convolution_convert_fusion = bf16[512,2048]{1,0:T(8,128)(2,1)} fusion(bf16[32,8,2048]{2,1,0:T(8,128)(2,1)} %all-to-all-done.4, s32[256]{0:T(256)S(1)} %all-reduce), kind=kOutput, calls=%fused_computation.3 | convolution fusion | flops 538050560 | bytes 3146752 | tf_op jit(solution)/shard_map/dot_general | solution.py:58
  202.7 5.6 %all-to-all-done.7 = bf16[32,16,256]{2,1,0:T(8,128)(2,1)S(1)} async-done(((bf16[32,16,256]{2,1,0:T(8,128)(2,1)}), bf16[32,16,256]{2,1,0:T(8,128)(2,1)S(1)}, u32[]{:S(2)}, u32[]{:S(2)}) %all-to-all-start.7) | async-done | bytes 262176 | tf_op jit(solution)/shard_map/all_to_all | solution.py:13
  208.3 4.6 %all-to-all-start.5 = ((bf16[32,16,2048]{2,1,0:T(8,128)(2,1)}), bf16[32,16,2048]{2,1,0:T(8,128)(2,1)}, u32[]{:S(2)}, u32[]{:S(2)}) async-start(bf16[32,16,2048]{2,1,0:T(8,128)(2,1)} %bitcast.63), calls=%async_computation.6 | async-start | bytes 4194304 | tf_op jit(solution)/shard_map/all_to_all | solution.py:13
  212.9 2.0 convolution_multiply_fusion
  214.9 3.6 %fusion.17 = f32[8,128,1024]{2,1,0:T(8,128)} fusion(bf16[8,128,64]{1,2,0:T(8,128)(2,1)} %get-tuple-element.5, bf16[8,64,1024]{2,1,0:T(8,128)(2,1)S(1)} %reshape.72), kind=kOutput, calls=%fused_computation.34 | convolution fusion | flops 134217728 | bytes 5373952 | tf_op jit(solution)/shard_map/bnr,brd->bnd/dot_general | solution.py:93
  218.6 0.8 reshape.87
  219.4 7.2 %fusion = bf16[1024,1024]{1,0:T(8,128)(2,1)} fusion(f32[8,128,1024]{2,1,0:T(8,128)} %fusion.17, bf16[1024,1024]{1,0:T(8,128)(2,1)} %all-gather.3.cloned.1.call-done, bf16[1024,1024]{1,0:T(8,128)(2,1)} %param.8), kind=kOutput, calls=%fused_computation.2 | convolution fusion | flops 2149580800 | bytes 10485760 | tf_op jit(solution)/shard_map/dot_general | solution.py:87
  226.5 14.7 %all-to-all-done.5 = bf16[32,16,2048]{2,1,0:T(8,128)(2,1)} async-done(((bf16[32,16,2048]{2,1,0:T(8,128)(2,1)}), bf16[32,16,2048]{2,1,0:T(8,128)(2,1)}, u32[]{:S(2)}, u32[]{:S(2)}) %all-to-all-start.5) | async-done | bytes 2097184 | tf_op jit(solution)/shard_map/all_to_all | solution.py:13
  241.3 4.1 %copy.34 = bf16[16,32,2048]{2,1,0:T(8,128)(2,1)} copy(bf16[16,32,2048]{2,0,1:T(8,128)(2,1)} %bitcast.19) | data formatting | bytes 4194304 | tf_op jit(solution)/shard_map/transpose | solution.py:24
  245.4 4.1 %reshape.83 = bf16[16,64,1024]{2,1,0:T(8,128)(2,1)} reshape(bf16[16,32,2048]{2,1,0:T(8,128)(2,1)} %copy.34) | data formatting | bytes 4194304 | tf_op jit(solution)/shard_map/reshape | solution.py:24
  249.5 1.8 fusion.5
  (25 shorter events, 1.0 us)
Async XLA Ops:
  7.2 1.6 copy-start
  7.2 212.2 %all-gather.3.cloned.1.call-start = ((), (), s32[]{:S(2)}) async-start(), calls=%async_computation.10 | async-start | bytes 2359296 | tf_op jit(solution)/shard_map/all_gather | solution.py:88
  7.9 241.6 %reduce-scatter.2.cloned.1.call-start = ((), (), s32[]{:S(2)}) async-start(), calls=%async_computation.9 | async-start | bytes 4718592 | tf_op jit(solution)/shard_map/reduce_scatter | solution.py:79
  14.6 0.9 copy-start.4
  16.5 17.6 %all-to-all-start.2 = ((bf16[32,16,256]{2,1,0:T(8,128)(2,1)}), bf16[32,16,256]{2,1,0:T(8,128)(2,1)S(1)}, u32[]{:S(2)}, u32[]{:S(2)}) async-start(bf16[32,16,256]{2,1,0:T(8,128)(2,1)} %copy.31), calls=%async_computation.3 | async-start | bytes 524288 | tf_op jit(solution)/shard_map/all_to_all | solution.py:13
  33.2 7.6 %copy-start.5 = (s32[8]{0:T(128)S(1)}, s32[8]{0:T(128)}, u32[]{:S(2)}) copy-start(s32[8]{0:T(128)} %param.11) | copy-start | bytes 100
  33.3 7.6 %copy-start.1 = (s32[512]{0:T(512)S(1)}, s32[512]{0:T(512)}, u32[]{:S(2)}) copy-start(s32[512]{0:T(512)} %param.12) | copy-start | bytes 6148
  33.3 8.3 %copy-start.6 = (u32[256]{0:T(256)S(1)}, u32[256]{0:T(256)}, u32[]{:S(2)}) copy-start(u32[256]{0:T(256)} %constant.12) | copy-start | bytes 3076
  34.1 41.6 %all-to-all-start = ((bf16[32,16,2048]{2,1,0:T(8,128)(2,1)}), bf16[32,16,2048]{2,1,0:T(8,128)(2,1)}, u32[]{:S(2)}, u32[]{:S(2)}) async-start(bf16[32,16,2048]{2,1,0:T(8,128)(2,1)} %copy.29), calls=%async_computation.1 | async-start | bytes 4194304 | tf_op jit(solution)/shard_map/all_to_all | solution.py:13
  75.7 14.7 %all-to-all-start.3 = ((bf16[32,8,256]{2,1,0:T(8,128)(2,1)}), bf16[32,8,256]{2,1,0:T(8,128)(2,1)S(1)}, u32[]{:S(2)}, u32[]{:S(2)}) async-start(bf16[32,8,256]{2,1,0:T(8,128)(2,1)} %fusion.3), calls=%async_computation.4 | async-start | bytes 262144 | tf_op jit(solution)/shard_map/all_to_all | solution.py:13
  85.9 10.1 %copy-start.2 = (bf16[1024,128]{1,0:T(8,128)(2,1)S(1)}, bf16[1024,128]{1,0:T(8,128)(2,1)}, u32[]{:S(2)}) copy-start(bf16[1024,128]{1,0:T(8,128)(2,1)} %param.13) | copy-start | bytes 786436
  90.4 21.0 %all-to-all-start.1 = ((bf16[32,8,2048]{2,1,0:T(8,128)(2,1)}), bf16[32,8,2048]{2,1,0:T(8,128)(2,1)S(1)}, u32[]{:S(2)}, u32[]{:S(2)}) async-start(bf16[32,8,2048]{2,1,0:T(8,128)(2,1)} %fusion.1), calls=%async_computation.2 | async-start | bytes 2097152 | tf_op jit(solution)/shard_map/all_to_all | solution.py:13
  152.9 18.5 %all-to-all-start.6 = ((bf16[32,8,256]{2,1,0:T(8,128)(2,1)}), bf16[32,8,256]{2,1,0:T(8,128)(2,1)S(1)}, u32[]{:S(2)}, u32[]{:S(2)}) async-start(bf16[32,8,256]{2,1,0:T(8,128)(2,1)} %bitcast.60), calls=%async_computation.7 | async-start | bytes 262144 | tf_op jit(solution)/shard_map/all_to_all | solution.py:13
  171.4 24.0 %all-to-all-start.4 = ((bf16[32,8,2048]{2,1,0:T(8,128)(2,1)}), bf16[32,8,2048]{2,1,0:T(8,128)(2,1)}, u32[]{:S(2)}, u32[]{:S(2)}) async-start(bf16[32,8,2048]{2,1,0:T(8,128)(2,1)} %bitcast.66), calls=%async_computation.5 | async-start | bytes 2097152 | tf_op jit(solution)/shard_map/all_to_all | solution.py:13
  195.4 13.0 %all-to-all-start.7 = ((bf16[32,16,256]{2,1,0:T(8,128)(2,1)}), bf16[32,16,256]{2,1,0:T(8,128)(2,1)S(1)}, u32[]{:S(2)}, u32[]{:S(2)}) async-start(bf16[32,16,256]{2,1,0:T(8,128)(2,1)} %bitcast.72), calls=%async_computation.8 | async-start | bytes 524288 | tf_op jit(solution)/shard_map/all_to_all | solution.py:13
  208.3 33.0 %all-to-all-start.5 = ((bf16[32,16,2048]{2,1,0:T(8,128)(2,1)}), bf16[32,16,2048]{2,1,0:T(8,128)(2,1)}, u32[]{:S(2)}, u32[]{:S(2)}) async-start(bf16[32,16,2048]{2,1,0:T(8,128)(2,1)} %bitcast.63), calls=%async_computation.6 | async-start | bytes 4194304 | tf_op jit(solution)/shard_map/all_to_all | solution.py:13
  245.4 4.1 %copy-start.3 = (f32[8,128,128]{2,1,0:T(8,128)S(1)}, f32[8,128,128]{2,1,0:T(8,128)}, u32[]{:S(2)}) copy-start(f32[8,128,128]{2,1,0:T(8,128)} %convolution_multiply_fusion) | copy-start | bytes 1572868
Sparse Core Ops, SparseCore 0:
  9.7 47.7 all-gather.2
  60.1 57.5 reduce-scatter.1

commit v2 on v1

v2 whole, which is shorter than its diff:
```python
import functools

import jax
import jax.numpy as jnp
from jax import lax
from jax.experimental import pallas as pl
from jax.experimental.pallas import tpu as pltpu
from jax.sharding import PartitionSpec as P

BLOCK = 128
MESH = pl.DeviceIdType.MESH
f32, bf16, i32 = jnp.float32, jnp.bfloat16, jnp.int32
adapter_scale = 0.5

NX, NY, NC, NZ = 4, 4, 2, 8
DP = NX * NY * NC


def nt(a, b):
    return lax.dot_general(a, b, (((1,), (1,)), ((), ())), preferred_element_type=f32)


def tn(a, b):
    return lax.dot_general(a, b, (((0,), (0,)), ((), ())), preferred_element_type=f32)


def nn(a, b):
    return jnp.dot(a, b, preferred_element_type=f32)


class Sems:
    def __init__(self, ref):
        self.ref, self.used = ref, 0

    def take(self):
        self.used += 1
        return self.ref.at[self.used - 1]


def kernel(
    apb,
    asi,
    x_hbm,
    w_hbm,
    d_hbm,
    u_hbm,
    dy_hbm,
    values_out,
    gi_out,
    gd_out,
    gu_out,
    sem_ref,
    xv,
    wv,
    uv,
    dyv,
    spot,
    spot_in,
    spot_all,
    spot_s,
    lu_s,
    ru,
    u_t,
    fu,
    ub,
    d1a1,
    d1a2,
    d1b1,
    d1b2,
    table,
    chosen,
    d2_t,
    bd,
    yv,
    rs_send,
    rs_recv,
    dyall,
    ar_part,
    ar_in,
    ar_mid,
    glt,
    lowt,
    lmat,
    term,
    g2_t,
    pieces,
    sums,
    g1_t,
    tu,
    su,
    ug_t,
    gu,
    guv,
    giv,
    valv,
):
    i = lax.axis_index("dp")
    z = lax.axis_index("tensor")
    c = lax.rem(i, NC)
    y = lax.rem(lax.div(i, NC), NY)
    x = lax.div(i, NC * NY)
    sems = Sems(sem_ref)

    def dev(xx=x, yy=y, cc=c, zz=z):
        return ((xx * NY + yy) * NC + cc, zz)

    def turn(v, d, n):
        return lax.rem(v + d, n)

    def remote(src, dst, device):
        copy = pltpu.make_async_remote_copy(
            src_ref=src,
            dst_ref=dst,
            send_sem=sems.take(),
            recv_sem=sems.take(),
            device_id=device,
            device_id_type=MESH,
        )
        copy.start()
        return copy

    def local(src, dst):
        copy = pltpu.make_async_copy(src, dst, sems.take())
        copy.start()
        return copy

    def wait(copies):
        for copy in copies:
            copy.wait()

    def step(axis, src, dst):
        own, size = {"x": (x, NX), "y": (y, NY), "c": (c, NC)}[axis]
        key = {"x": "xx", "y": "yy", "c": "cc"}[axis]
        copies = []
        for d in (1, 3, 2) if size == 4 else (1,):
            to = turn(own, d, size)
            copies.append(remote(src(to), dst(own), dev(**{key: to})))
        copies.append(local(src(own), dst(own)))
        return copies

    class Exchange:
        def __init__(self, slots, mid, out):
            self.slots, self.mid, self.out = slots, mid, out

        def first(self):
            s, m = self.slots, self.mid
            self.copies = step("x", lambda t: s.at[t, :, :, 0], lambda o: m.at[0, o]) + step(
                "y", lambda t: s.at[:, t, :, 1], lambda o: m.at[1, :, o]
            )

        def second(self):
            wait(self.copies)
            m = self.mid
            self.copies = step("y", lambda t: m.at[0, :, t], lambda o: m.at[2, :, o]) + step(
                "x", lambda t: m.at[1, t], lambda o: m.at[3, o]
            )

        def third(self):
            wait(self.copies)
            m, out = self.mid, self.out
            self.copies = step("c", lambda t: m.at[2, :, :, t], lambda o: out.at[:, :, o, 0]) + step(
                "c", lambda t: m.at[3, :, :, t], lambda o: out.at[:, :, o, 1]
            )

        def finish(self):
            wait(self.copies)

    def lanes(k, width):
        return pl.ds(pl.multiple_of(k * width, width), width)

    class Down:
        def first(self):
            self.copies = step(
                "x",
                lambda t: d_hbm.at[pl.ds(0, 8), :, :, :, lanes(t, 256)],
                lambda o: d1a1.at[o],
            ) + step("y", lambda t: d_hbm.at[pl.ds(8, 8), t], lambda o: d1b1.at[o])

        def second(self):
            wait(self.copies)
            self.copies = step("y", lambda t: d1a1.at[:, :, t], lambda o: d1a2.at[:, o]) + step(
                "x", lambda t: d1b1.at[:, :, :, :, lanes(t, 256)], lambda o: d1b2.at[o]
            )

        def third(self):
            wait(self.copies)
            self.copies = step("c", lambda t: d1a2.at[:, :, :, t], lambda o: table.at[o, 0]) + step(
                "c", lambda t: d1b2.at[:, :, :, t], lambda o: table.at[o, 1]
            )

        def finish(self):
            wait(self.copies)

    class Gather:
        def slot(self, k):
            return dyall.at[lax.div(k, 2), :, lanes(lax.rem(k, 2), BLOCK)]

        def start(self, s):
            self.copies = []
            for d, last in ((1, 4), (NZ - 1, 3)):
                if s < last:
                    k = turn(z, (NZ - d) * s, NZ)
                    src = dyv if s == 0 else self.slot(k)
                    self.copies.append(remote(src, self.slot(k), dev(zz=turn(z, d, NZ))))
            if s == 0:
                self.own = local(dyv, self.slot(z))

        def finish(self, s):
            wait(self.copies)
            if s == 0:
                self.own.wait()

    class Scatter:
        def start(self, s):
            if s:
                wait(self.copies)
            self.copies = []
            for way, (d, last) in enumerate(((1, 4), (NZ - 1, 3))):
                if s < last:
                    own = yv[turn(z, d * (last - s), NZ)]
                    if s:
                        own = own + rs_recv[way, s - 1].astype(f32)
                    rs_send[way, s] = own.astype(bf16)
                    self.copies.append(
                        remote(rs_send.at[way, s], rs_recv.at[way, s], dev(zz=turn(z, d, NZ)))
                    )

        def finish(self):
            wait(self.copies)

    class Reduce:
        def __init__(self, k, out, scale):
            self.k, self.out, self.scale = k, out, scale

        def first(self):
            k = self.k
            self.copies = [
                remote(
                    ar_part.at[k, turn(z, d, NZ)],
                    ar_in.at[k, d - 1],
                    dev(zz=turn(z, d, NZ)),
                )
                for d in range(1, NZ)
            ]

        def second(self):
            k = self.k
            wait(self.copies)
            total = ar_part[k, z]
            for d in range(1, NZ):
                total = total + ar_in[k, d - 1]
            ar_mid[k] = (total * self.scale).astype(bf16)
            self.copies = [
                remote(ar_mid.at[k], self.out.at[z], dev(zz=turn(z, d, NZ))) for d in range(1, NZ)
            ] + [local(ar_mid.at[k], self.out.at[z])]

        def finish(self):
            wait(self.copies)

    barrier = pltpu.get_barrier_semaphore()
    peers = [dev(xx=turn(x, d, NX)) for d in range(1, NX)]
    peers += [dev(yy=turn(y, d, NY)) for d in range(1, NY)]
    peers += [dev(cc=turn(c, 1, NC))]
    peers += [dev(zz=turn(z, d, NZ)) for d in range(1, NZ)]
    for device in peers:
        pl.semaphore_signal(barrier, inc=1, device_id=device, device_id_type=MESH)
    load_dy = local(dy_hbm, dyv)
    load_u = local(u_hbm, uv)
    load_x = local(x_hbm, xv)
    load_w = local(w_hbm, wv)

    lane = lax.broadcasted_iota(i32, (8, 256), 1)
    mine = jnp.zeros((8, 256), i32)
    for b in range(8):
        mine = jnp.where(lane == i * 8 + b, asi[apb[b]], mine)
    spot[0] = mine
    pl.semaphore_wait(barrier, len(peers))

    down = Down()
    gather = Gather()
    scatter = Scatter()

    axes = (("xx", x, NX), ("yy", y, NY), ("cc", c, NC))
    for k, (key, own, size) in enumerate(axes):
        copies = [
            remote(spot.at[k], spot_in.at[3 * k + d - 1], dev(**{key: turn(own, d, size)}))
            for d in range(1, size)
        ]
        if k == 0:
            down.first()
            load_dy.wait()
            gather.start(0)
        wait(copies)
        total = spot[k]
        for d in range(1, size):
            total = total + spot_in[3 * k + d - 1]
        if k < 2:
            spot[k + 1] = total
        else:
            spot_all[...] = total
    local(spot_all, spot_s).wait()

    load_u.wait()

    def reply(k, _):
        found = jnp.int32(0)
        for b in range(8):
            s = spot_s[0, k * 8 + b]
            hit = lax.shift_right_logical(s, 4) == i
            found = jnp.where(hit, lax.bitwise_and(s, 15) + 1, found)
        lu_s[k] = found - 1
        chunk = uv[jnp.maximum(found - 1, 0)]
        ru[lax.div(k, 8), lax.rem(lax.div(k, 2), 4), lax.rem(k, 2)] = chunk
        return 0

    lax.fori_loop(0, DP, reply, 0)
    up = Exchange(ru, u_t, fu)
    up.first()

    load_x.wait()
    load_w.wait()

    def base(n, _):
        part = nn(xv[...], wv[:, lanes(n, 256)])
        yv[2 * n] = part[:, :BLOCK]
        yv[2 * n + 1] = part[:, BLOCK:]
        return 0

    lax.fori_loop(0, 4, base, 0)

    gather.finish(0)
    gather.start(1)
    down.second()
    up.second()
    gather.finish(1)
    gather.start(2)
    up.third()
    up.finish()

    for b in range(8):
        k = lax.shift_right_logical(spot_s[0, i * 8 + b], 4)
        chunk = fu[
            lax.shift_right_logical(k, 3),
            lax.bitwise_and(lax.shift_right_logical(k, 1), 3),
            lax.bitwise_and(k, 1),
        ]
        ub[b] = chunk.reshape(64, BLOCK)
    for b in range(8):
        ar_part[0, b] = nt(ub[b], dyv[b * BLOCK : (b + 1) * BLOCK])
    grad_low = Reduce(0, glt, adapter_scale)
    grad_low.first()

    gather.finish(2)
    gather.start(3)
    grad_low.second()
    down.third()
    down.finish()

    def choose(k, _):
        for b in range(8):
            s = spot_s[0, k * 8 + b]
            piece = table[
                lax.bitwise_and(lax.shift_right_logical(s, 4), 1),
                lax.bitwise_and(lax.shift_right_logical(s, 3), 1),
                lax.shift_right_logical(s, 7),
                lax.bitwise_and(lax.shift_right_logical(s, 5), 3),
                lax.bitwise_and(s, 7),
            ]
            chosen[lax.div(k, 8), lax.rem(lax.div(k, 2), 4), lax.rem(k, 2), b // 4, b % 4] = piece
        return 0

    lax.fori_loop(0, DP, choose, 0)
    fetch = Exchange(chosen, d2_t, bd)
    fetch.first()

    grad_low.finish()
    row = lax.broadcasted_iota(i32, (512, 64), 0)
    col = lax.broadcasted_iota(i32, (512, 64), 1)
    for b in range(8):
        spread = (row == col * 8 + b).astype(f32).astype(bf16)
        lmat[:, b * BLOCK : (b + 1) * BLOCK] = nn(spread, glt[b]).astype(bf16)

    def terms(n, _):
        part = nn(lmat[...], xv[:, lanes(n, 256)])
        term[:, :, :, :, :, lanes(n, 256)] = part.reshape(4, 4, 2, 2, 8, 256).astype(bf16)
        return 0

    lax.fori_loop(0, 4, terms, 0)
    give = Exchange(term, g2_t, pieces)
    give.first()

    fetch.second()
    gather.finish(3)
    scatter.start(0)
    give.second()
    fetch.third()
    fetch.finish()

    for b in range(8):
        part = jnp.zeros((64, BLOCK), f32)
        for q in range(4):
            mat = bd[q, :, :, b // 4, b % 4].reshape(64, 256)
            part = part + nt(mat, xv[b * BLOCK : (b + 1) * BLOCK, q * 256 : (q + 1) * 256])
        ar_part[1, b] = part
    low = Reduce(1, lowt, 1.0)
    low.first()
    scatter.start(1)
    give.third()
    give.finish()

    pick = (lax.broadcasted_iota(i32, (512, 256), 0) == spot_all[0:1, :]).astype(f32).astype(bf16)

    def add(n, _):
        for h in range(2):
            mat = pieces[:, :, :, h, :, lanes(n, 256)].reshape(256, 256)
            part = nn(pick, mat).astype(bf16)
            sums[:, :, :, h, :, lanes(n, 256)] = part.reshape(4, 4, 2, 16, 256)
        return 0

    lax.fori_loop(0, 4, add, 0)
    keep = Exchange(sums, g1_t, gd_out)
    keep.first()

    low.second()
    scatter.start(2)
    low.finish()
    for b in range(8):
        tu[b] = nn(lowt[b], dyv[b * BLOCK : (b + 1) * BLOCK]).astype(bf16).reshape(2, 32, BLOCK)

    def send_up(k, _):
        found = jnp.int32(0)
        for b in range(8):
            hit = lax.shift_right_logical(spot_s[0, i * 8 + b], 4) == k
            found = jnp.where(hit, b + 1, found)
        chunk = tu[jnp.maximum(found - 1, 0)].astype(f32)
        chunk = jnp.where(found > 0, chunk, 0.0)
        su[lax.div(k, 8), lax.rem(lax.div(k, 2), 4), lax.rem(k, 2)] = chunk.astype(bf16)
        return 0

    lax.fori_loop(0, DP, send_up, 0)
    give_up = Exchange(su, ug_t, gu)
    give_up.first()

    def backward(n, _):
        part = jnp.zeros((1024, 256), f32)
        for k in range(4):
            part = part + nt(dyall[k], wv[lanes(n, 256), k * 256 : (k + 1) * 256])
        for b in range(8):
            rows = slice(b * BLOCK, (b + 1) * BLOCK)
            mat = bd[n, :, :, b // 4, b % 4].reshape(64, 256)
            giv[rows, lanes(n, 256)] = (part[rows] + tn(glt[b], mat)).astype(bf16)
        return 0

    lax.fori_loop(0, 4, backward, 0)
    store_gi = local(giv, gi_out)
    scatter.start(3)
    keep.second()
    give_up.second()
    give_up.third()
    give_up.finish()

    def add_up(k, _):
        def one(j, total):
            chunk = gu[lax.div(j, 8), lax.rem(lax.div(j, 2), 4), lax.rem(j, 2)].astype(f32)
            return total + jnp.where(lu_s[j] == k, chunk, 0.0)

        total = lax.fori_loop(0, DP, one, jnp.zeros((2, 32, BLOCK), f32))
        guv[k] = total.astype(bf16)
        return 0

    lax.fori_loop(0, 16, add_up, 0)
    store_gu = local(guv, gu_out)
    scatter.finish()
    for b in range(8):
        rows = slice(b * BLOCK, (b + 1) * BLOCK)
        frozen = yv[z, rows] + rs_recv[0, 3, rows].astype(f32) + rs_recv[1, 2, rows].astype(f32)
        valv[rows] = (frozen + adapter_scale * tn(lowt[b], ub[b])).astype(bf16)
    store_values = local(valv, values_out)
    keep.third()
    keep.finish()
    wait([store_gi, store_gu, store_values])
    assert sems.used <= sem_ref.shape[0], sems.used


def on_device(inputs, frozen, down, up, apb, asi, dy):
    any_ = pl.BlockSpec(memory_space=pl.ANY)
    smem = pl.BlockSpec(memory_space=pltpu.SMEM)

    def v(*shape, dtype=bf16):
        return pltpu.VMEM(shape, dtype)

    values, grad_inputs, gd, gu = pl.pallas_call(
        kernel,
        out_shape=(
            jax.ShapeDtypeStruct((1024, 128), bf16),
            jax.ShapeDtypeStruct((1024, 1024), bf16),
            jax.ShapeDtypeStruct((4, 4, 2, 2, 16, 1024), bf16),
            jax.ShapeDtypeStruct((16, 2, 32, 128), bf16),
        ),
        in_specs=[smem, smem, any_, any_, any_, any_, any_],
        out_specs=(any_,) * 4,
        scratch_shapes=[
            pltpu.SemaphoreType.DMA((340,)),
            v(1024, 1024),
            v(1024, 1024),
            v(16, 2, 32, 128),
            v(1024, 128),
            v(3, 8, 256, dtype=i32),
            v(7, 8, 256, dtype=i32),
            v(8, 256, dtype=i32),
            pltpu.SMEM((8, 256), i32),
            pltpu.SMEM((32,), i32),
            v(4, 4, 2, 2, 32, 128),
            v(4, 4, 4, 2, 32, 128),
            v(4, 4, 2, 2, 32, 128),
            v(8, 64, 128),
            v(4, 8, 4, 2, 8, 256),
            v(4, 4, 8, 2, 8, 256),
            v(4, 8, 2, 8, 1024),
            v(4, 4, 8, 2, 8, 256),
            v(2, 2, 4, 4, 8, 8, 256),
            v(4, 4, 2, 2, 4, 8, 256),
            v(4, 4, 4, 2, 4, 8, 256),
            v(4, 4, 2, 2, 4, 8, 256),
            v(8, 1024, 128, dtype=f32),
            v(2, 4, 1024, 128),
            v(2, 4, 1024, 128),
            v(4, 1024, 256),
            v(2, 8, 64, 128, dtype=f32),
            v(2, 7, 64, 128, dtype=f32),
            v(2, 64, 128),
            v(8, 64, 128),
            v(8, 64, 128),
            v(512, 1024),
            v(4, 4, 2, 2, 8, 1024),
            v(4, 4, 4, 2, 8, 1024),
            v(4, 4, 2, 2, 8, 1024),
            v(4, 4, 2, 2, 16, 1024),
            v(4, 4, 4, 2, 16, 1024),
            v(8, 2, 32, 128),
            v(4, 4, 2, 2, 32, 128),
            v(4, 4, 4, 2, 32, 128),
            v(4, 4, 2, 2, 32, 128),
            v(16, 2, 32, 128),
            v(1024, 1024),
            v(1024, 128),
        ],
        compiler_params=pltpu.CompilerParams(
            collective_id=0, has_side_effects=True, vmem_limit_bytes=60 * 2**20
        ),
    )(
        apb,
        asi,
        inputs,
        frozen,
        down.swapaxes(1, 2).reshape(16, 4, 2, 8, 1024),
        up.reshape(16, 2, 32, 128),
        dy,
    )
    grad_down = gd.reshape(64, 16, 1024).transpose(1, 2, 0)
    return values, grad_inputs, grad_down, gu.reshape(16, 64, 128)


def solution(mesh):
    return jax.shard_map(
        on_device,
        mesh=mesh,
        in_specs=(
            P("dp", "tensor"),
            P("tensor", None),
            P("dp", "tensor", None),
            P("dp", None, "tensor"),
            P("dp"),
            P(),
            P("dp", "tensor"),
        ),
        out_specs=(
            P("dp", "tensor"),
            P("dp", "tensor"),
            P("dp", "tensor", None),
            P("dp", None, "tensor"),
        ),
        check_vma=False,
    )
```

time: 260 us -> 149 us (0.57)
  Pallas kernels: 0 us -> 141 us
  blocking collectives: 65.2 us -> 0 us
  waiting for transfers between devices: 57 us -> 0 us
  starting transfers between devices: 52.5 us -> 0 us
  matrix products: 34 us -> 0 us
  local copies, waits for them, and re-layouts: 32.6 us -> 6.95 us
  between operations: 14.9 us -> 0.66 us
    pallas_call x0 -> x1, Pallas kernels: none -> 141 us  [on_device(): pl.pallas_call(kernel, out_shape=(jax.ShapeDtypeStruct((1024, 128), bf16)...]
    all_to_all x8 -> x0, waiting for transfers between devices: 56.3 us -> none  [exchange(): return lax.all_to_all(pieces, 'dp', split_axis=0, concat_axis=0, tiled=True)]
    all_to_all x8 -> x0, starting transfers between devices: 52.5 us -> none  [exchange(): return lax.all_to_all(pieces, 'dp', split_axis=0, concat_axis=0, tiled=True)]
    dot_general x12 -> x0, matrix products: 34 us -> none  [the longest x1 7.15 us: on_device(): lax.dot_general(lax.all_gather(value_gradient, 'tensor', axis=1, tiled=Tr...]
    psum x1 -> x0, blocking collectives: 33.5 us -> none  [on_device(): low = lax.psum(low_part, 'tensor').astype(bf16)]
    unnamed x1 -> x0, blocking collectives: 31.7 us -> none
    reshape x10 -> x1, local copies, waits for them, and re-layouts: 18.1 us -> 4.21 us  [on_device(): grad_down = gd.reshape(64, 16, 1024).transpose(1, 2, 0)]
    transpose x6 -> x0, local copies, waits for them, and re-layouts: 11.3 us -> none  [the longest x4 6.4 us: join(): return pieces.swapaxes(0, 1).reshape(m, parts * (size // width), width)]
  transfers between devices with their start and end apart: 10 -> 0, of which waited for: 7 -> 0; matrix products, arithmetic and copies ran while one was open for 25% -> 0% of each run, Pallas kernels for 0% -> 0%
where the time goes in v2:
time: 149 us
  Pallas kernels  141 us (95%)
  local copies, waits for them, and re-layouts  6.95 us (5%)
    pallas_call x1, Pallas kernels, on_device(): pl.pallas_call(kernel, out_shape=(jax.ShapeDtypeStruct((1024, 128), bf16)...  141 us
    reshape x1, local copies, waits for them, and re-layouts, on_device(): grad_down = gd.reshape(64, 16, 1024).transpose(1, 2, 0)  4.21 us

profile of v2, /device:TPU:1, one launch (start us, length us, event | category | flops | bytes accessed | tf_op | source)
XLA Modules:
  0.0 149.1 jit_solution(18363957693704962364)
XLA Ops:
  0.6 141.5 %shard_map.102 = (bf16[1024,128]{1,0:T(8,128)(2,1)}, bf16[1024,1024]{1,0:T(8,128)(2,1)}, bf16[4,4,2,2,16,1024]{5,4,3,2,1,0:T(8,128)(2,1)}, bf16[16,2,32,128]{3,2,1,0:T(8,128)(2,1)}) custom-call(s32[8]{0:T(128)} %apb.1, s32[512]{0:T(512)} %asi.1, bf16[1024,1024]{1,0:T(8,128)(2,1)} %x_hbm.1, bf16[1024,1024]{1,0:T(8,128)(2,1)} %w_hbm.1, ...), custom_call_target="tpu_custom_call" | custom-call | tf_op jit(solution)/shard_map/pallas_call | solution.py:492
  142.1 0.0 copy-start.2
  142.1 0.0 copy-start
  142.1 4.2 %copy.13 = bf16[64,16,1024]{2,0,1:T(8,128)(2,1)} copy(bf16[64,16,1024]{2,1,0:T(8,128)(2,1)} %bitcast.11) | data formatting | bytes 4194304 | tf_op jit(solution)/shard_map/reshape | solution.py:560
  146.3 0.0 copy-done.2
  146.3 0.7 copy.17
  147.0 0.0 copy-done
  147.0 0.0 copy-start.1
  147.0 1.3 copy.18
  148.4 0.0 copy-done.1
  148.4 0.7 copy.19
Async XLA Ops:
  142.1 4.2 %copy-start.2 = (bf16[1024,128]{1,0:T(8,128)(2,1)S(1)}, bf16[1024,128]{1,0:T(8,128)(2,1)}, u32[]{:S(2)}) copy-start(bf16[1024,128]{1,0:T(8,128)(2,1)} %get-tuple-element.16) | copy-start | bytes 786436
  142.1 4.9 %copy-start = (bf16[1024,1024]{1,0:T(8,128)(2,1)S(1)}, bf16[1024,1024]{1,0:T(8,128)(2,1)}, u32[]{:S(2)}) copy-start(bf16[1024,1024]{1,0:T(8,128)(2,1)} %get-tuple-element.17) | copy-start | bytes 6291460
  147.0 1.3 copy-start.1

commit v3 on v2

--- a/solution.py
+++ b/solution.py
@@ -316,6 +316,9 @@
     lax.fori_loop(0, DP, reply, 0)
     up = Exchange(ru, u_t, fu)
     up.first()
+    down.second()
+    gather.finish(0)
+    gather.start(1)
 
     load_x.wait()
     load_w.wait()
@@ -327,10 +330,6 @@
         return 0
 
     lax.fori_loop(0, 4, base, 0)
-
-    gather.finish(0)
-    gather.start(1)
-    down.second()
     up.second()
     gather.finish(1)
     gather.start(2)
@@ -349,11 +348,8 @@
         ar_part[0, b] = nt(ub[b], dyv[b * BLOCK : (b + 1) * BLOCK])
     grad_low = Reduce(0, glt, adapter_scale)
     grad_low.first()
-
-    gather.finish(2)
-    gather.start(3)
+    down.third()
     grad_low.second()
-    down.third()
     down.finish()
 
     def choose(k, _):
@@ -388,12 +384,14 @@
     lax.fori_loop(0, 4, terms, 0)
     give = Exchange(term, g2_t, pieces)
     give.first()
-
+    gather.finish(2)
+    gather.start(3)
     fetch.second()
+    pick = (lax.broadcasted_iota(i32, (512, 256), 0) == spot_all[0:1, :]).astype(f32).astype(bf16)
+    give.second()
+    fetch.third()
     gather.finish(3)
     scatter.start(0)
-    give.second()
-    fetch.third()
     fetch.finish()
 
     for b in range(8):
@@ -404,11 +402,8 @@
         ar_part[1, b] = part
     low = Reduce(1, lowt, 1.0)
     low.first()
-    scatter.start(1)
     give.third()
     give.finish()
-
-    pick = (lax.broadcasted_iota(i32, (512, 256), 0) == spot_all[0:1, :]).astype(f32).astype(bf16)
 
     def add(n, _):
         for h in range(2):
@@ -422,7 +417,7 @@
     keep.first()
 
     low.second()
-    scatter.start(2)
+    scatter.start(1)
     low.finish()
     for b in range(8):
         tu[b] = nn(lowt[b], dyv[b * BLOCK : (b + 1) * BLOCK]).astype(bf16).reshape(2, 32, BLOCK)
@@ -440,6 +435,9 @@
     lax.fori_loop(0, DP, send_up, 0)
     give_up = Exchange(su, ug_t, gu)
     give_up.first()
+    scatter.start(2)
+    give_up.second()
+    keep.second()
 
     def backward(n, _):
         part = jnp.zeros((1024, 256), f32)
@@ -453,18 +451,15 @@
 
     lax.fori_loop(0, 4, backward, 0)
     store_gi = local(giv, gi_out)
+    give_up.third()
     scatter.start(3)
-    keep.second()
-    give_up.second()
-    give_up.third()
     give_up.finish()
 
     def add_up(k, _):
-        def one(j, total):
-            chunk = gu[lax.div(j, 8), lax.rem(lax.div(j, 2), 4), lax.rem(j, 2)].astype(f32)
-            return total + jnp.where(lu_s[j] == k, chunk, 0.0)
-
-        total = lax.fori_loop(0, DP, one, jnp.zeros((2, 32, BLOCK), f32))
+        total = jnp.zeros((2, 32, BLOCK), f32)
+        for j in range(DP):
+            share = jnp.where(lu_s[j] == k, 1.0, 0.0).astype(f32)
+            total = total + gu[j // 8, (j // 2) % 4, j % 2].astype(f32) * share
         guv[k] = total.astype(bf16)
         return 0
 

time: 149 us -> 134 us (0.90)
  Pallas kernels: 141 us -> 127 us
    pallas_call x1, Pallas kernels: 141 us -> 127 us  [on_device(): pl.pallas_call(kernel, out_shape=(jax.ShapeDtypeStruct((1024, 128), bf16)...]
where the time goes in v3:
time: 134 us
  Pallas kernels  127 us (95%)
  local copies, waits for them, and re-layouts  6.95 us (5%)
    pallas_call x1, Pallas kernels, on_device(): pl.pallas_call(kernel, out_shape=(jax.ShapeDtypeStruct((1024, 128), bf16)...  127 us
    reshape x1, local copies, waits for them, and re-layouts, on_device(): grad_down = gd.reshape(64, 16, 1024).transpose(1, 2, 0)  4.21 us
    unnamed x9, local copies, waits for them, and re-layouts  2.74 us

profile of v3, /device:TPU:1, one launch (start us, length us, event | category | flops | bytes accessed | tf_op | source)
XLA Modules:
  0.0 134.2 jit_solution(6186854745186800534)
XLA Ops:
  0.6 126.6 %shard_map.102 = (bf16[1024,128]{1,0:T(8,128)(2,1)}, bf16[1024,1024]{1,0:T(8,128)(2,1)}, bf16[4,4,2,2,16,1024]{5,4,3,2,1,0:T(8,128)(2,1)}, bf16[16,2,32,128]{3,2,1,0:T(8,128)(2,1)}) custom-call(s32[8]{0:T(128)} %apb.1, s32[512]{0:T(512)} %asi.1, bf16[1024,1024]{1,0:T(8,128)(2,1)} %x_hbm.1, bf16[1024,1024]{1,0:T(8,128)(2,1)} %w_hbm.1, ...), custom_call_target="tpu_custom_call" | custom-call | tf_op jit(solution)/shard_map/pallas_call | solution.py:487
  127.2 0.0 copy-start.2
  127.2 0.0 copy-start
  127.3 4.2 %copy.13 = bf16[64,16,1024]{2,0,1:T(8,128)(2,1)} copy(bf16[64,16,1024]{2,1,0:T(8,128)(2,1)} %bitcast.11) | data formatting | bytes 4194304 | tf_op jit(solution)/shard_map/reshape | solution.py:555
  131.5 0.0 copy-done.2
  131.5 0.7 copy.17
  132.2 0.0 copy-done
  132.2 0.0 copy-start.1
  132.2 1.3 copy.18
  133.5 0.0 copy-done.1
  133.5 0.7 copy.19
Async XLA Ops:
  127.2 4.2 %copy-start.2 = (bf16[1024,128]{1,0:T(8,128)(2,1)S(1)}, bf16[1024,128]{1,0:T(8,128)(2,1)}, u32[]{:S(2)}) copy-start(bf16[1024,128]{1,0:T(8,128)(2,1)} %get-tuple-element.16) | copy-start | bytes 786436
  127.2 4.9 %copy-start = (bf16[1024,1024]{1,0:T(8,128)(2,1)S(1)}, bf16[1024,1024]{1,0:T(8,128)(2,1)}, u32[]{:S(2)}) copy-start(bf16[1024,1024]{1,0:T(8,128)(2,1)} %get-tuple-element.17) | copy-start | bytes 6291460
  132.2 1.3 copy-start.1

commit v4 on v3

--- a/solution.py
+++ b/solution.py
@@ -132,7 +132,7 @@
         own, size = {"x": (x, NX), "y": (y, NY), "c": (c, NC)}[axis]
         key = {"x": "xx", "y": "yy", "c": "cc"}[axis]
         copies = []
-        for d in (1, 3, 2) if size == 4 else (1,):
+        for d in (2, 1, 3) if size == 4 else (1,):
             to = turn(own, d, size)
             copies.append(remote(src(to), dst(own), dev(**{key: to})))
         copies.append(local(src(own), dst(own)))
@@ -142,25 +142,30 @@
         def __init__(self, slots, mid, out):
             self.slots, self.mid, self.out = slots, mid, out
 
-        def first(self):
+            self.halves = [[], []]
+
+        def first(self, *halves):
             s, m = self.slots, self.mid
-            self.copies = step("x", lambda t: s.at[t, :, :, 0], lambda o: m.at[0, o]) + step(
-                "y", lambda t: s.at[:, t, :, 1], lambda o: m.at[1, :, o]
-            )
+            for h in halves or (0, 1):
+                if h == 0:
+                    self.halves[0] = step("x", lambda t: s.at[t, :, :, 0], lambda o: m.at[0, o])
+                else:
+                    self.halves[1] = step("y", lambda t: s.at[:, t, :, 1], lambda o: m.at[1, :, o])
 
         def second(self):
-            wait(self.copies)
-            m = self.mid
-            self.copies = step("y", lambda t: m.at[0, :, t], lambda o: m.at[2, :, o]) + step(
-                "x", lambda t: m.at[1, t], lambda o: m.at[3, o]
-            )
+            m, (one, two) = self.mid, self.halves
+            wait(one)
+            one = step("y", lambda t: m.at[0, :, t], lambda o: m.at[2, :, o])
+            wait(two)
+            self.halves = one, step("x", lambda t: m.at[1, t], lambda o: m.at[3, o])
 
         def third(self):
-            wait(self.copies)
-            m, out = self.mid, self.out
-            self.copies = step("c", lambda t: m.at[2, :, :, t], lambda o: out.at[:, :, o, 0]) + step(
-                "c", lambda t: m.at[3, :, :, t], lambda o: out.at[:, :, o, 1]
-            )
+            m, out, (one, two) = self.mid, self.out, self.halves
+            wait(one)
+            one = step("c", lambda t: m.at[2, :, :, t], lambda o: out.at[:, :, o, 0])
+            wait(two)
+            two = step("c", lambda t: m.at[3, :, :, t], lambda o: out.at[:, :, o, 1])
+            self.copies = one + two
 
         def finish(self):
             wait(self.copies)
@@ -170,26 +175,29 @@
 
     class Down:
         def first(self):
-            self.copies = step(
+            self.one = step(
                 "x",
                 lambda t: d_hbm.at[pl.ds(0, 8), :, :, :, lanes(t, 256)],
                 lambda o: d1a1.at[o],
-            ) + step("y", lambda t: d_hbm.at[pl.ds(8, 8), t], lambda o: d1b1.at[o])
+            )
+            self.two = step("y", lambda t: d_hbm.at[pl.ds(8, 8), t], lambda o: d1b1.at[o])
 
         def second(self):
-            wait(self.copies)
-            self.copies = step("y", lambda t: d1a1.at[:, :, t], lambda o: d1a2.at[:, o]) + step(
+            wait(self.two)
+            self.two = step(
                 "x", lambda t: d1b1.at[:, :, :, :, lanes(t, 256)], lambda o: d1b2.at[o]
             )
+            wait(self.one)
+            self.one = step("y", lambda t: d1a1.at[:, :, t], lambda o: d1a2.at[:, o])
 
         def third(self):
-            wait(self.copies)
-            self.copies = step("c", lambda t: d1a2.at[:, :, :, t], lambda o: table.at[o, 0]) + step(
-                "c", lambda t: d1b2.at[:, :, :, t], lambda o: table.at[o, 1]
-            )
+            wait(self.two)
+            self.two = step("c", lambda t: d1b2.at[:, :, :, t], lambda o: table.at[o, 1])
+            wait(self.one)
+            self.one = step("c", lambda t: d1a2.at[:, :, :, t], lambda o: table.at[o, 0])
 
         def finish(self):
-            wait(self.copies)
+            wait(self.one + self.two)
 
     class Gather:
         def slot(self, k):
@@ -352,22 +360,24 @@
     grad_low.second()
     down.finish()
 
-    def choose(k, _):
-        for b in range(8):
-            s = spot_s[0, k * 8 + b]
-            piece = table[
-                lax.bitwise_and(lax.shift_right_logical(s, 4), 1),
-                lax.bitwise_and(lax.shift_right_logical(s, 3), 1),
-                lax.shift_right_logical(s, 7),
-                lax.bitwise_and(lax.shift_right_logical(s, 5), 3),
-                lax.bitwise_and(s, 7),
-            ]
-            chosen[lax.div(k, 8), lax.rem(lax.div(k, 2), 4), lax.rem(k, 2), b // 4, b % 4] = piece
-        return 0
-
-    lax.fori_loop(0, DP, choose, 0)
     fetch = Exchange(chosen, d2_t, bd)
-    fetch.first()
+    for h in range(2):
+
+        def choose(k, _):
+            for b in range(4):
+                s = spot_s[0, k * 8 + h * 4 + b]
+                piece = table[
+                    lax.bitwise_and(lax.shift_right_logical(s, 4), 1),
+                    lax.bitwise_and(lax.shift_right_logical(s, 3), 1),
+                    lax.shift_right_logical(s, 7),
+                    lax.bitwise_and(lax.shift_right_logical(s, 5), 3),
+                    lax.bitwise_and(s, 7),
+                ]
+                chosen[lax.div(k, 8), lax.rem(lax.div(k, 2), 4), lax.rem(k, 2), h, b] = piece
+            return 0
+
+        lax.fori_loop(0, DP, choose, 0)
+        fetch.first(h)
 
     grad_low.finish()
     row = lax.broadcasted_iota(i32, (512, 64), 0)
@@ -405,16 +415,17 @@
     give.third()
     give.finish()
 
-    def add(n, _):
-        for h in range(2):
+    keep = Exchange(sums, g1_t, gd_out)
+    for h in range(2):
+
+        def add(n, _):
             mat = pieces[:, :, :, h, :, lanes(n, 256)].reshape(256, 256)
             part = nn(pick, mat).astype(bf16)
             sums[:, :, :, h, :, lanes(n, 256)] = part.reshape(4, 4, 2, 16, 256)
-        return 0
-
-    lax.fori_loop(0, 4, add, 0)
-    keep = Exchange(sums, g1_t, gd_out)
-    keep.first()
+            return 0
+
+        lax.fori_loop(0, 4, add, 0)
+        keep.first(h)
 
     low.second()
     scatter.start(1)
@@ -435,10 +446,6 @@
     lax.fori_loop(0, DP, send_up, 0)
     give_up = Exchange(su, ug_t, gu)
     give_up.first()
-    scatter.start(2)
-    give_up.second()
-    keep.second()
-
     def backward(n, _):
         part = jnp.zeros((1024, 256), f32)
         for k in range(4):
@@ -451,6 +458,10 @@
 
     lax.fori_loop(0, 4, backward, 0)
     store_gi = local(giv, gi_out)
+    scatter.start(2)
+    give_up.second()
+    keep.second()
+
     give_up.third()
     scatter.start(3)
     give_up.finish()

time: 134 us -> 136 us (1.015)
  no operation moved by 1% of the time
where the time goes in v4:
time: 136 us; the launch traced here: 135 us
  Pallas kernels  128 us (94%)
  local copies, waits for them, and re-layouts  6.95 us (5%)
    pallas_call x1, Pallas kernels, on_device(): pl.pallas_call(kernel, out_shape=(jax.ShapeDtypeStruct((1024, 128), bf16)...  128 us
    reshape x1, local copies, waits for them, and re-layouts, on_device(): grad_down = gd.reshape(64, 16, 1024).transpose(1, 2, 0)  4.21 us
    unnamed x9, local copies, waits for them, and re-layouts  2.74 us

profile of v4, /device:TPU:1, one launch (start us, length us, event | category | flops | bytes accessed | tf_op | source)
XLA Modules:
  0.0 135.4 jit_solution(641484481826971012)
XLA Ops:
  0.6 127.8 %shard_map.102 = (bf16[1024,128]{1,0:T(8,128)(2,1)}, bf16[1024,1024]{1,0:T(8,128)(2,1)}, bf16[4,4,2,2,16,1024]{5,4,3,2,1,0:T(8,128)(2,1)}, bf16[16,2,32,128]{3,2,1,0:T(8,128)(2,1)}) custom-call(s32[8]{0:T(128)} %apb.1, s32[512]{0:T(512)} %asi.1, bf16[1024,1024]{1,0:T(8,128)(2,1)} %x_hbm.1, bf16[1024,1024]{1,0:T(8,128)(2,1)} %w_hbm.1, ...), custom_call_target="tpu_custom_call" | custom-call | tf_op jit(solution)/shard_map/pallas_call | solution.py:498
  128.4 0.0 copy-start.2
  128.4 0.0 copy-start
  128.5 4.2 %copy.13 = bf16[64,16,1024]{2,0,1:T(8,128)(2,1)} copy(bf16[64,16,1024]{2,1,0:T(8,128)(2,1)} %bitcast.11) | data formatting | bytes 4194304 | tf_op jit(solution)/shard_map/reshape | solution.py:566
  132.7 0.0 copy-done.2
  132.7 0.7 copy.17
  133.4 0.0 copy-done
  133.4 0.0 copy-start.1
  133.4 1.3 copy.18
  134.7 0.0 copy-done.1
  134.7 0.7 copy.19
Async XLA Ops:
  128.4 4.2 %copy-start.2 = (bf16[1024,128]{1,0:T(8,128)(2,1)S(1)}, bf16[1024,128]{1,0:T(8,128)(2,1)}, u32[]{:S(2)}) copy-start(bf16[1024,128]{1,0:T(8,128)(2,1)} %get-tuple-element.16) | copy-start | bytes 786436
  128.4 4.9 %copy-start = (bf16[1024,1024]{1,0:T(8,128)(2,1)S(1)}, bf16[1024,1024]{1,0:T(8,128)(2,1)}, u32[]{:S(2)}) copy-start(bf16[1024,1024]{1,0:T(8,128)(2,1)} %get-tuple-element.17) | copy-start | bytes 6291460
  133.4 1.3 copy-start.1
